TPU v7x, 512 devices: a whole 4x4x16 slice. The times are simulated.
512 devices in a mesh: pair: 64 (over z, x), int: 8 (over y, core).
Axes of the slice: x: 4, y: 4, z: 16, core: 2. Of those that a mesh axis runs over, the one named last changes fastest.
Arguments:
- amps: bfloat16 [512, 64, 4096], P('pair', None, 'int'), may hold values from -6 to 6
- amp_mask: int32 [512, 64], P('pair'), may hold values 0 or 1
- integrals: bfloat16 [64, 4096, 4096], P('pair', None, 'int'), may hold values from -0.09375 to 0.09375
- block_mask: int32 [64], P('pair'), may hold values 0 or 1
- in_tiles: int32 [64], replicated, may hold values from 0 to 63, each once
- out_tiles: int32 [64], replicated, may hold values from 0 to 63, each once
- vir_energy: float32 [1024], replicated, may hold values from 0.5 to 3
- pair_energy: float32 [512], P('pair'), may hold values from -4 to -1
- dressing: bfloat16 [1024, 1024], P('pair'), may hold values from -0.1875 to 0.1875
Outputs:
- new_amps: bfloat16 [512, 64, 4096], P('pair', None, 'int')
Inputs may be any that keep to these rules, and one draw needn't show every extreme that they name: `in_tiles`: a permutation of the 64 tiles. `out_tiles`: a permutation of the 64 tiles.
All inputs are finite; a program needn't handle non-finite values. No bound on the sum of `amp_mask` or of `block_mask` on one device may be relied on, other than what follows from the above.
Results may differ from a plain program's by a relative error of at most 0.0038.
Values may be sent and summed in bfloat16 or wider, within the bound.
A program may use at most 64 MiB of HBM per device.

v0:
```python
import jax
import jax.numpy as jnp
from jax import lax
from jax.sharding import PartitionSpec as P

TILE = 64
VT = 16
WA = 4


def shards(
    amps, amp_mask, integrals, block_mask, in_tiles, out_tiles, vir_energy, pair_energy, dressing
):
    local_pairs, tile_count, share_size = amps.shape
    strip_rows = share_size // TILE
    int_index = lax.axis_index("int")
    masked = jnp.where(amp_mask[:, :, None] > 0, amps, jnp.zeros_like(amps))
    ordered = jnp.take(masked, in_tiles, axis=1)
    received = lax.all_to_all(ordered, "pair", split_axis=1, concat_axis=0, tiled=True)
    partial_value = jnp.einsum(
        "psk,sak->psa", received, integrals, preferred_element_type=jnp.float32
    )
    partial_value = partial_value * block_mask.astype(jnp.float32)[None, :, None]
    partial_value = lax.optimization_barrier(partial_value.astype(jnp.bfloat16)).astype(jnp.float32)
    summed = lax.psum(partial_value.astype(jnp.bfloat16), "int").astype(jnp.float32)
    own_share = lax.dynamic_slice_in_dim(summed, int_index * share_size, share_size, 2)
    returned = lax.all_to_all(
        own_share.astype(jnp.bfloat16), "pair", split_axis=0, concat_axis=1, tiled=True
    ).astype(own_share.dtype)
    slot_of = (
        jnp.zeros((tile_count,), jnp.int32)
        .at[out_tiles]
        .set(jnp.arange(tile_count, dtype=jnp.int32))
    )
    ladder_terms = jnp.take(returned, slot_of, axis=1)
    tile_rows = masked.reshape(local_pairs, WA, VT, strip_rows, TILE)
    tile_rows = jnp.transpose(tile_rows, (0, 1, 3, 2, 4)).reshape(
        local_pairs * WA * strip_rows, VT * TILE
    )
    running = jnp.dot(
        tile_rows,
        lax.all_gather(dressing, "pair", axis=0, tiled=True),
        preferred_element_type=jnp.float32,
    )
    running = running.reshape(local_pairs, WA, strip_rows, VT, TILE)
    cycle_terms = jnp.transpose(running, (0, 1, 3, 2, 4)).reshape(
        local_pairs, tile_count, share_size
    )
    energies = vir_energy.reshape(VT, TILE)
    own_energy = lax.dynamic_slice_in_dim(energies[:WA], int_index * strip_rows, strip_rows, 1)
    denominator = (
        pair_energy[:, None, None, None, None]
        - own_energy[None, :, None, :, None]
        - energies[None, None, :, None, :]
    )
    denominator = denominator.reshape(local_pairs, tile_count, share_size)
    updated = masked.astype(jnp.float32) + (ladder_terms + cycle_terms) / denominator
    return updated.astype(jnp.bfloat16)


def solution(mesh):
    in_specs = (
        P("pair", None, "int"),
        P("pair", None),
        P("pair", None, "int"),
        P("pair"),
        P(),
        P(),
        P(),
        P("pair"),
        P("pair", None),
    )
    out_specs = P("pair", None, "int")
    return jax.shard_map(shards, mesh=mesh, in_specs=in_specs, out_specs=out_specs, check_vma=False)
```

profile of v0, /device:TPU:16, one launch (start us, length us, event | category | flops | bytes accessed | tf_op | source)
XLA Modules:
  0.0 241.5 jit_solution(16358082051121928171)
XLA Ops:
  7.4 0.7 broadcast_compare_fusion
  8.2 0.7 compare_and_fusion
  8.8 0.7 compare_select_fusion
  9.5 1.4 copy_select_fusion
  10.9 0.6 gather_fusion
  11.5 0.9 select_bitcast_fusion
  12.4 18.6 %all-to-all-start = ((bf16[8,64,512]{2,0,1:T(8,128)(2,1)}), bf16[8,64,512]{2,0,1:T(8,128)(2,1)S(1)}, u32[]{:S(2)}, u32[]{:S(2)}) async-start(bf16[8,64,512]{2,0,1:T(8,128)(2,1)} %select_bitcast_fusion), calls=%async_computation | async-start | bytes 1048576 | tf_op jit(solution)/shard_map/all_to_all | solution.py:19
  31.7 32.1 %all-to-all-done = bf16[8,64,512]{2,0,1:T(8,128)(2,1)S(1)} async-done(((bf16[8,64,512]{2,0,1:T(8,128)(2,1)}), bf16[8,64,512]{2,0,1:T(8,128)(2,1)S(1)}, u32[]{:S(2)}, u32[]{:S(2)}) %all-to-all-start) | async-done | bytes 524320 | tf_op jit(solution)/shard_map/all_to_all | solution.py:19
  63.8 6.5 %fusion = bf16[512,1,4096]{2,0,1:T(8,128)(2,1)} fusion(bf16[1,4096,512]{2,1,0:T(8,128)(2,1)} %param.11, f32[]{:T(128)} %bitcast.5, bf16[8,64,512]{2,0,1:T(8,128)(2,1)S(1)} %all-to-all-done), kind=kOutput, calls=%fused_computation.4 | convolution fusion | flops 2151677952 | bytes 8912900 | tf_op jit(solution)/shard_map/psk,sak->psa/dot_general | solution.py:20
  70.4 0.5 all-gather.2.cloned.1.call-update
  70.9 75.6 %all-reduce.2.cloned.1.call-done = bf16[512,1,4096]{2,0,1:T(8,128)(2,1)} async-done(((bf16[512,1,4096]{2,0,1:T(8,128)(2,1)}), bf16[512,1,4096]{2,0,1:T(8,128)(2,1)}) %all-reduce.2.cloned.1.call-update) | async-done | bytes 4194320 | tf_op jit(solution)/shard_map/psum | solution.py:25
  146.6 1.1 convert_convert_fusion
  147.7 0.5 broadcast.65
  148.2 1.0 reduce
  149.2 1.0 reshape.101
  150.2 15.8 %all-to-all-start.1 = ((bf16[64,2,2048]{2,1,0:T(2,128)(2,1)}), bf16[64,2,2048]{2,1,0:T(2,128)(2,1)}, u32[]{:S(2)}, u32[]{:S(2)}) async-start(bf16[64,2,2048]{2,1,0:T(2,128)(2,1)} %reshape.101), calls=%async_computation.1 | async-start | bytes 1048576 | tf_op jit(solution)/shard_map/all_to_all | solution.py:27
  166.0 1.5 reshape.65
  167.8 0.3 sub.43
  168.1 0.5 sub.44
  168.6 2.4 %copy.21 = bf16[8,4,8,16,64]{4,3,2,1,0:T(8,128)(2,1)S(1)} copy(bf16[8,4,8,16,64]{4,2,0,3,1:T(8,128)(2,1)} %bitcast.60) | data formatting | bytes 1048576 | tf_op jit(solution)/shard_map/transpose | solution.py:37
  171.1 1.5 reshape.96
  172.6 0.1 sub.47
  172.7 1.0 scatter_custom_fusion
  173.7 42.3 %all-gather.2.cloned.1.call-done = bf16[1024,1024]{1,0:T(8,128)(2,1)} async-done(((bf16[16,1024]{1,0:T(8,128)(2,1)}), bf16[1024,1024]{1,0:T(8,128)(2,1)}) %all-gather.2.cloned.1.call-update) | async-done | bytes 2097168 | tf_op jit(solution)/shard_map/all_gather | solution.py:42
  216.0 2.9 %copy.22 = bf16[1024,1024]{1,0:T(8,128)(2,1)S(1)} copy(bf16[1024,1024]{0,1:T(8,128)(2,1)} %bitcast.61) | data formatting | bytes 4194304 | tf_op jit(solution)/shard_map/dot_general | solution.py:40
  218.9 3.7 %convolution_bitcast_fusion = f32[8,4,16,8,64]{4,3,2,1,0:T(8,128)} fusion(bf16[16,64,1024,1,1]{2,1,0,4,3:T(8,128)(2,1)S(1)} %bitcast.62, bf16[8,4,8,1024,1]{3,2,1,0,4:T(8,128)(2,1)} %reshape.96), kind=kOutput, calls=%fused_computation.6 | convolution fusion | flops 536870912 | bytes 3670016 | tf_op jit(solution)/shard_map/dot_general | solution.py:40
  222.6 1.9 reshape.66
  224.5 3.6 %reshape.102 = bf16[512,1,512]{2,1,0:T(2,128)(2,1)S(1)} reshape(bf16[64,2,2048]{2,1,0:T(2,128)(2,1)} %all-to-all-done.1) | data formatting | bytes 1048576
  228.1 1.1 copy.33
  229.2 1.8 gather_fusion.1
  231.1 2.1 fusion.4
  233.1 0.9 copy.24
  (21 shorter events, 0.6 us)
Async XLA Ops:
  12.4 51.4 %all-to-all-start = ((bf16[8,64,512]{2,0,1:T(8,128)(2,1)}), bf16[8,64,512]{2,0,1:T(8,128)(2,1)S(1)}, u32[]{:S(2)}, u32[]{:S(2)}) async-start(bf16[8,64,512]{2,0,1:T(8,128)(2,1)} %select_bitcast_fusion), calls=%async_computation | async-start | bytes 1048576 | tf_op jit(solution)/shard_map/all_to_all | solution.py:19
  31.0 115.6 %all-reduce.2.cloned.1.call-start = ((), (), s32[]{:S(2)}) async-start(), calls=%async_computation.2 | async-start | bytes 8388608 | tf_op jit(solution)/shard_map/psum | solution.py:25
  70.3 97.2 %copy-start = (f32[1024]{0:T(1024)S(1)}, f32[1024]{0:T(1024)}, u32[]{:S(2)}) copy-start(f32[1024]{0:T(1024)} %param.15) | copy-start | bytes 12292
  70.3 97.3 %slice-start = ((f32[1024]{0:T(1024)}), f32[256]{0:T(256)S(1)}, s32[]{:S(2)}) async-start(f32[1024]{0:T(1024)} %param.15), calls=%async_computation.4 | async-start | bytes 2048 | tf_op jit(solution)/shard_map/slice | solution.py:50
  70.3 97.4 %copy-start.1 = (f32[8]{0:T(128)S(1)}, f32[8]{0:T(128)}, u32[]{:S(2)}) copy-start(f32[8]{0:T(128)} %param.16) | copy-start | bytes 100
  70.4 145.7 %all-gather.2.cloned.1.call-start = ((), (), s32[]{:S(2)}) async-start(), calls=%async_computation.3 | async-start | bytes 2129920 | tf_op jit(solution)/shard_map/all_gather | solution.py:42
  150.2 74.3 %all-to-all-start.1 = ((bf16[64,2,2048]{2,1,0:T(2,128)(2,1)}), bf16[64,2,2048]{2,1,0:T(2,128)(2,1)}, u32[]{:S(2)}, u32[]{:S(2)}) async-start(bf16[64,2,2048]{2,1,0:T(2,128)(2,1)} %reshape.101), calls=%async_computation.1 | async-start | bytes 1048576 | tf_op jit(solution)/shard_map/all_to_all | solution.py:27
Sparse Core Ops, SparseCore 0:
  70.5 76.0 all-reduce.1
Sparse Core Ops, SparseCore 1:
  73.8 142.2 all-gather.1
where the time goes:
time: 242 us
  waiting for transfers between devices  151 us (62%)
  starting transfers between devices  34.4 us (14%)
  local copies, waits for them, and re-layouts  22.1 us (9%)
  between operations  15.6 us (6%)
  matrix products  10.2 us (4%)
  other arithmetic  8.61 us (4%)
    psum x1, waiting for transfers between devices, shards(): lax.psum(partial_value.astype(jnp.bfloat16), 'int').astype(jnp.float32)  75.6 us
    all_gather x1, waiting for transfers between devices, shards(): lax.all_gather(dressing, 'pair', axis=0, tiled=True)  42.3 us
    all_to_all x1, waiting for transfers between devices, shards(): lax.all_to_all(ordered, 'pair', split_axis=1, concat_axis=0, tiled=True)  32.1 us
    all_to_all x1, starting transfers between devices, shards(): lax.all_to_all(ordered, 'pair', split_axis=1, concat_axis=0, tiled=True)  18.6 us
    all_to_all x1, starting transfers between devices, shards(): lax.all_to_all(own_share.astype(jnp.bfloat16), 'pair', split_axis=0, conc...  15.8 us
    dot_general x1, matrix products, shards(): jnp.einsum('psk,sak->psa', received, integrals, preferred_element_type=jn...  6.51 us
    unnamed x7, local copies, waits for them, and re-layouts  5.7 us
  transfers between devices with their start and end apart: 4, of which 3 were waited for; matrix products, arithmetic and copies ran while one was open for 8% of the time, Pallas kernels for 0%

commit v1 on v0

--- a/solution.py
+++ b/solution.py
@@ -6,6 +6,11 @@
 TILE = 64
 VT = 16
 WA = 4
+
+
+def swapped_in(x, axis, along):
+    stack = jnp.stack([x] * lax.axis_size(axis))
+    return jnp.concatenate(lax.all_to_all(stack, axis, 0, 0), axis=along)
 
 
 def shards(
@@ -38,9 +43,7 @@
         local_pairs * WA * strip_rows, VT * TILE
     )
     running = jnp.dot(
-        tile_rows,
-        lax.all_gather(dressing, "pair", axis=0, tiled=True),
-        preferred_element_type=jnp.float32,
+        tile_rows, swapped_in(dressing, "pair", 0), preferred_element_type=jnp.float32
     )
     running = running.reshape(local_pairs, WA, strip_rows, VT, TILE)
     cycle_terms = jnp.transpose(running, (0, 1, 3, 2, 4)).reshape(

time: 242 us -> 326 us (1.35)
  the two profiles are of different devices: /device:TPU:16 before, /device:TPU:24 now
where the time goes in v1:
time: 326 us; the launch traced here: 325 us
  waiting for transfers between devices  188 us (58%)
  blocking collectives  48.6 us (15%)
  local copies, waits for them, and re-layouts  30.5 us (9%)
  starting transfers between devices  24.8 us (8%)
  between operations  14.2 us (4%)
  matrix products  10.9 us (3%)
  other arithmetic  8.61 us (3%)
    all_to_all x1, waiting for transfers between devices, swapped_in(): return jnp.concatenate(lax.all_to_all(stack, axis, 0, 0), axis=along)  78.8 us
    psum x1, waiting for transfers between devices, shards(): lax.psum(partial_value.astype(jnp.bfloat16), 'int').astype(jnp.float32)  76.8 us
    all_to_all x1, blocking collectives, shards(): lax.all_to_all(own_share.astype(jnp.bfloat16), 'pair', split_axis=0, conc...  48.6 us
    all_to_all x1, waiting for transfers between devices, shards(): lax.all_to_all(ordered, 'pair', split_axis=1, concat_axis=0, tiled=True)  32.1 us
    all_to_all x1, starting transfers between devices, shards(): lax.all_to_all(ordered, 'pair', split_axis=1, concat_axis=0, tiled=True)  18.6 us
    unnamed x11, local copies, waits for them, and re-layouts  6.98 us
  transfers between devices with their start and end apart: 3, of which 3 were waited for; matrix products, arithmetic and copies ran while one was open for 7% of the time, Pallas kernels for 0%

profile of v1, /device:TPU:24, one launch (start us, length us, event | category | flops | bytes accessed | tf_op | source)
XLA Modules:
  0.0 325.4 jit_solution(5936950947498881350)
XLA Ops:
  6.5 0.7 broadcast_compare_fusion
  7.3 0.7 compare_and_fusion
  8.0 0.7 compare_select_fusion
  8.7 1.4 copy_select_fusion
  10.1 0.6 gather_fusion
  10.7 0.9 select_bitcast_fusion
  11.6 18.6 %all-to-all-start = ((bf16[8,64,512]{2,0,1:T(8,128)(2,1)}), bf16[8,64,512]{2,0,1:T(8,128)(2,1)S(1)}, u32[]{:S(2)}, u32[]{:S(2)}) async-start(bf16[8,64,512]{2,0,1:T(8,128)(2,1)} %select_bitcast_fusion), calls=%async_computation | async-start | bytes 1048576 | tf_op jit(solution)/shard_map/all_to_all | solution.py:24
  30.9 32.1 %all-to-all-done = bf16[8,64,512]{2,0,1:T(8,128)(2,1)S(1)} async-done(((bf16[8,64,512]{2,0,1:T(8,128)(2,1)}), bf16[8,64,512]{2,0,1:T(8,128)(2,1)S(1)}, u32[]{:S(2)}, u32[]{:S(2)}) %all-to-all-start) | async-done | bytes 524320 | tf_op jit(solution)/shard_map/all_to_all | solution.py:24
  63.0 6.5 %fusion = bf16[512,1,4096]{2,0,1:T(8,128)(2,1)} fusion(bf16[1,4096,512]{2,1,0:T(8,128)(2,1)} %param.11, f32[]{:T(128)} %bitcast.5, bf16[8,64,512]{2,0,1:T(8,128)(2,1)S(1)} %all-to-all-done), kind=kOutput, calls=%fused_computation.4 | convolution fusion | flops 2151677952 | bytes 8912900 | tf_op jit(solution)/shard_map/psk,sak->psa/dot_general | solution.py:25
  69.5 76.8 %all-reduce.2.cloned.1.call-done = bf16[512,1,4096]{2,0,1:T(8,128)(2,1)} async-done(((bf16[512,1,4096]{2,0,1:T(8,128)(2,1)}), bf16[512,1,4096]{2,0,1:T(8,128)(2,1)}) %all-reduce.2.cloned.1.call-update) | async-done | bytes 4194320 | tf_op jit(solution)/shard_map/psum | solution.py:30
  146.4 1.1 convert_convert_fusion
  147.4 0.5 broadcast.67
  147.9 1.0 reduce
  149.0 0.2 reshape.107
  149.2 48.6 %all_to_all.29 = bf16[64,2,2048]{2,1,0:T(2,128)(2,1)} all-to-all(bf16[64,2,2048]{2,1,0:T(2,128)(2,1)S(1)} %reshape.107), channel_id=1, replica_groups=mesh['pair'=64,'int'=8] {'pair'}, dimensions={0} | all-to-all | bytes 1048576 | tf_op jit(solution)/shard_map/all_to_all | solution.py:32
  197.8 1.6 stack.2
  199.4 6.2 %all-to-all-start.2 = ((bf16[64,16,1024]{2,1,0:T(8,128)(2,1)}), bf16[64,16,1024]{2,1,0:T(8,128)(2,1)S(1)}, u32[]{:S(2)}, u32[]{:S(2)}) async-start(bf16[64,16,1024]{2,1,0:T(8,128)(2,1)} %stack.2), calls=%async_computation.2 | async-start | bytes 4194304 | tf_op jit(solution)/shard_map/all_to_all | solution.py:13
  205.7 1.5 reshape.70
  207.5 1.6 sub.43
  209.1 1.9 sub.44
  211.1 3.4 %copy.21 = bf16[8,4,8,16,64]{4,3,2,1,0:T(8,128)(2,1)} copy(bf16[8,4,8,16,64]{4,2,0,3,1:T(8,128)(2,1)} %bitcast.63) | data formatting | bytes 1048576 | tf_op jit(solution)/shard_map/transpose | solution.py:42
  214.5 2.6 reshape.102
  217.3 1.0 scatter_custom_fusion
  218.3 4.5 %reshape.108 = bf16[512,1,512]{2,1,0:T(2,128)(2,1)} reshape(bf16[64,2,2048]{2,1,0:T(2,128)(2,1)} %all_to_all.29) | data formatting | bytes 1048576
  222.7 2.3 copy.33
  225.0 2.8 gather_fusion.1
  227.8 78.8 %all-to-all-done.2 = bf16[64,16,1024]{2,1,0:T(8,128)(2,1)S(1)} async-done(((bf16[64,16,1024]{2,1,0:T(8,128)(2,1)}), bf16[64,16,1024]{2,1,0:T(8,128)(2,1)S(1)}, u32[]{:S(2)}, u32[]{:S(2)}) %all-to-all-start.2) | async-done | bytes 2097184 | tf_op jit(solution)/shard_map/all_to_all | solution.py:13
  306.6 2.6 copy.22
  309.2 4.4 %convolution_bitcast_fusion = f32[8,4,16,8,64]{4,3,2,1,0:T(8,128)} fusion(bf16[16,64,1024,1,1]{2,1,0,4,3:T(8,128)(2,1)} %bitcast.64, bf16[8,4,8,1024,1]{3,2,1,0,4:T(8,128)(2,1)} %reshape.102), kind=kOutput, calls=%fused_computation.6 | convolution fusion | flops 536870912 | bytes 3670016 | tf_op jit(solution)/shard_map/dot_general | solution.py:45
  313.6 1.9 reshape.72
  315.6 2.1 fusion.4
  317.6 0.9 copy.24
  (24 shorter events, 0.6 us)
Async XLA Ops:
  11.6 51.4 %all-to-all-start = ((bf16[8,64,512]{2,0,1:T(8,128)(2,1)}), bf16[8,64,512]{2,0,1:T(8,128)(2,1)S(1)}, u32[]{:S(2)}, u32[]{:S(2)}) async-start(bf16[8,64,512]{2,0,1:T(8,128)(2,1)} %select_bitcast_fusion), calls=%async_computation | async-start | bytes 1048576 | tf_op jit(solution)/shard_map/all_to_all | solution.py:24
  30.2 116.2 %all-reduce.2.cloned.1.call-start = ((), (), s32[]{:S(2)}) async-start(), calls=%async_computation.3 | async-start | bytes 8388608 | tf_op jit(solution)/shard_map/psum | solution.py:30
  69.5 128.3 %copy-start.1 = (bf16[16,1024]{1,0:T(8,128)(2,1)S(1)}, bf16[16,1024]{1,0:T(8,128)(2,1)}, u32[]{:S(2)}) copy-start(bf16[16,1024]{1,0:T(8,128)(2,1)} %param.17) | copy-start | bytes 98308
  197.8 9.4 %copy-start.2 = (f32[1024]{0:T(1024)S(1)}, f32[1024]{0:T(1024)}, u32[]{:S(2)}) copy-start(f32[1024]{0:T(1024)} %param.15) | copy-start | bytes 12292
  197.8 9.5 %slice-start = ((f32[1024]{0:T(1024)}), f32[256]{0:T(256)S(1)}, s32[]{:S(2)}) async-start(f32[1024]{0:T(1024)} %param.15), calls=%async_computation.4 | async-start | bytes 2048 | tf_op jit(solution)/shard_map/slice | solution.py:53
  197.8 9.6 %copy-start.3 = (f32[8]{0:T(128)S(1)}, f32[8]{0:T(128)}, u32[]{:S(2)}) copy-start(f32[8]{0:T(128)} %param.16) | copy-start | bytes 100
  199.4 107.2 %all-to-all-start.2 = ((bf16[64,16,1024]{2,1,0:T(8,128)(2,1)}), bf16[64,16,1024]{2,1,0:T(8,128)(2,1)S(1)}, u32[]{:S(2)}, u32[]{:S(2)}) async-start(bf16[64,16,1024]{2,1,0:T(8,128)(2,1)} %stack.2), calls=%async_computation.2 | async-start | bytes 4194304 | tf_op jit(solution)/shard_map/all_to_all | solution.py:13
  309.2 6.4 %copy-start = (f32[64,8,512]{2,1,0:T(8,128)S(1)}, f32[64,8,512]{2,1,0:T(8,128)}, u32[]{:S(2)}) copy-start(f32[64,8,512]{2,1,0:T(8,128)} %gather_fusion.1) | copy-start | bytes 3145732
Sparse Core Ops, SparseCore 0:
  69.6 76.6 all-reduce.1
